TPU v7x, 32 devices: a whole 2x2x4 slice. The times are simulated.
32 devices in a mesh: space: 4 (over y, x), slot: 8 (over z, core).
Axes of the slice: x: 2, y: 2, z: 4, core: 2. Of those that a mesh axis runs over, the one named last changes fastest.
Arguments:
- control: bfloat16 [1536, 1024], P('slot', 'space'), may hold values from -6 to 6
- block_lists: int32 [32, 2], P('space'), may hold values from 0 to 7, all different within a row; in each aligned block of 8 rows (0 to 7, 8 to 15, ...) at most 2 rows name the same one
- loc_tiles: bfloat16 [32, 2, 128, 128], P('space'), may hold values from -0.375 to 0.375
- ensemble: bfloat16 [8, 1536, 4096], P('slot', None, 'space'), may hold values from -2.5 to 2.5
- obs_col: int32 [8, 8192], P('slot', 'space'), may hold values from 0 to 4095, as said below
- obs_wts: float32 [8, 48, 8192], P('slot', None, 'space'), may hold values from -0.875 to 0.875
- innovation: float32 [8, 8192], P('slot', 'space'), may hold values from -6 to 6
- inv_error: float32 [8, 8192], P('slot', 'space'), may hold values from 1 to 16
Outputs:
- first_grad: float32 [1536, 1024], P('slot', 'space')
- second_grad: float32 [1536, 1024], P('slot', 'space')
Inputs may be any that keep to these rules, and one draw needn't show every extreme that they name: `block_lists`: each grid block lists 2 different control blocks; among the grid blocks of one space index no control block is listed more than twice. `obs_col`: observation j lies in grid columns (j // 2048) * 8 * 128 to that plus 8 * 128 - 1.
All inputs are finite; a program needn't handle non-finite values.
Results may differ from a plain program's by a relative error of at most 0.0003.
Values may be sent and summed in bfloat16 or wider, within the bound.
A program may use at most 64 MiB of HBM per device.

v0:
```python
import jax
import jax.numpy as jnp
from jax import lax
from jax.sharding import PartitionSpec as P

LEV = 48
BLOCK = 128
K = 2
descent_step = 0.5


def per_device(control, block_lists, loc_tiles, ensemble, obs_col, obs_wts, innovation, inv_error):
    member_rows = control.shape[0]
    cell_count = ensemble.shape[2]
    space_count = lax.axis_size("space")
    block_total = control.shape[1] // BLOCK * space_count
    ref_ids = block_lists.reshape(-1)
    tiles_wide = loc_tiles.astype(jnp.float32)
    tiles_flat = tiles_wide.reshape(-1, BLOCK, BLOCK)
    selector = (ref_ids[:, None] == jnp.arange(block_total, dtype=jnp.int32)[None, :]).astype(
        jnp.float32
    )
    local_cols = obs_col[0] - lax.axis_index("space") * cell_count
    pick_table = (jnp.arange(cell_count, dtype=jnp.int32)[:, None] == local_cols[None, :]).astype(
        jnp.float32
    )
    weights = obs_wts[0]
    inverse = inv_error[0]
    observed = innovation[0]
    own_slot = ensemble[0]

    def localize(current):
        gathered = lax.all_gather(current.astype(jnp.float32), "space", axis=1, tiled=True)
        picked = gathered.reshape(member_rows, block_total, BLOCK)[:, ref_ids, :]
        products = jnp.einsum("crj,rij->cri", picked, tiles_flat, precision=lax.Precision.HIGHEST)
        return (
            products.reshape(member_rows, -1, K, BLOCK).sum(axis=2).reshape(member_rows, cell_count)
        )

    def observe(increment):
        seen_values = jnp.dot(increment, pick_table, precision=lax.Precision.HIGHEST)
        modelled = jnp.sum(weights * seen_values, axis=0)
        residual = inverse * (modelled - observed)
        return jnp.dot(weights * residual[None, :], pick_table.T, precision=lax.Precision.HIGHEST)

    def gradient(current):
        updates = localize(current)
        all_updates = lax.all_gather(updates, "slot", axis=0, tiled=True)
        product_full = own_slot.astype(jnp.float32) * all_updates
        increment = jnp.sum(product_full.reshape(-1, LEV, cell_count), axis=0)
        adjoint_obs = observe(increment)
        forcing = lax.psum_scatter(
            own_slot.astype(jnp.float32)
            * jnp.tile(adjoint_obs, (member_rows * lax.axis_size("slot") // LEV, 1)),
            "slot",
            scatter_dimension=0,
            tiled=True,
        )
        grid_cells = forcing.reshape(member_rows, -1, BLOCK)
        products = jnp.einsum(
            "cgi,gkij->cgkj", grid_cells, tiles_wide, precision=lax.Precision.HIGHEST
        )
        control_term = jnp.einsum(
            "rb,crj->cbj",
            selector,
            products.reshape(member_rows, -1, BLOCK),
            precision=lax.Precision.HIGHEST,
        )
        returned = lax.psum_scatter(
            control_term.reshape(member_rows, block_total * BLOCK),
            "space",
            scatter_dimension=1,
            tiled=True,
        )
        return current.astype(jnp.float32) + returned

    first_grad = gradient(control)
    stepped = control.astype(jnp.float32) - descent_step * first_grad
    second_grad = gradient(stepped)
    return (first_grad, second_grad)


def solution(mesh):
    placed = (
        P("slot", "space"),
        P("space", None),
        P("space", None, None, None),
        P("slot", None, "space"),
        P("slot", "space"),
        P("slot", None, "space"),
        P("slot", "space"),
        P("slot", "space"),
    )
    return jax.shard_map(
        per_device,
        mesh=mesh,
        in_specs=placed,
        out_specs=(P("slot", "space"), P("slot", "space")),
        check_vma=False,
    )
```

profile of v0, /device:TPU:0, one launch (start us, length us, event | category | flops | bytes accessed | tf_op | source)
XLA Modules:
  0.0 419.0 jit_solution(14871258517747074934)
XLA Ops:
  7.2 0.8 copy.38
  8.1 0.9 convert_element_type.7
  9.0 12.7 %all_gather.12 = f32[192,1024]{1,0:T(8,128)S(1)} all-gather(f32[192,256]{1,0:T(8,128)S(1)} %convert_element_type.7), channel_id=1, replica_groups=mesh['space'=4,'slot'=8] {'space'}, dimensions={1}, use_global_device_ids=true | all-gather | bytes 983040 | tf_op jit(solution)/shard_map/all_gather | solution.py:33
  22.4 1.1 bitcast_reduce_fusion.1
  23.6 1.0 copy_bitcast_fusion.3
  24.6 65.1 %all-gather.3.cloned.1.call-done = f32[1536,1024]{1,0:T(8,128)} async-done(((f32[192,1024]{1,0:T(8,128)}), f32[1536,1024]{1,0:T(8,128)}) %all-gather.3.cloned.1.call-update) | async-done | bytes 6291472 | tf_op jit(solution)/shard_map/all_gather | solution.py:48
  89.8 8.0 %convert_multiply_fusion.3 = f32[1536,1024]{1,0:T(8,128)} fusion(f32[1536,1024]{1,0:T(8,128)} %all-gather.3.cloned.1.call-done, bf16[1,1536,1024]{2,1,0:T(8,128)(2,1)} %param.11), kind=kLoop, calls=%fused_computation.5 | loop fusion | flops 3145728 | bytes 15728640 | tf_op jit(solution)/shard_map/mul | solution.py:49
  97.8 3.2 reduce_sum.59
  101.1 3.2 fusion.19
  104.3 4.2 %fusion.2 = f32[48,1024]{1,0:T(8,128)S(1)} fusion(s32[2048]{0:T(1024)S(1)} %bitcast.114, f32[1,48,2048]{2,1,0:T(8,128)S(1)} %copy-done.7, f32[2048]{0:T(1024)S(1)} %bitcast.119), kind=kOutput, calls=%fused_computation.9 | convolution fusion | flops 1210155008 | bytes 606208 | tf_op jit(solution)/shard_map/dot_general | solution.py:44
  108.5 3.6 convert_multiply_fusion.2
  112.4 68.3 %reduce-scatter.5.cloned.1.call-done = f32[192,1024]{1,0:T(8,128)} async-done(((f32[1536,1024]{1,0:T(8,128)}), f32[192,1024]{1,0:T(8,128)}) %reduce-scatter.5.cloned.1.call-update) | async-done | bytes 786448 | tf_op jit(solution)/shard_map/reduce_scatter | solution.py:52
  180.7 1.3 copy.58
  182.8 1.5 fusion.16
  184.3 1.0 copy.77
  185.4 24.6 %reduce-scatter.7.cloned.1.call-done = f32[192,256]{1,0:T(8,128)} async-done(((f32[192,1024]{1,0:T(8,128)}), f32[192,256]{1,0:T(8,128)}) %reduce-scatter.7.cloned.1.call-update) | async-done | bytes 196624 | tf_op jit(solution)/shard_map/reduce_scatter | solution.py:69
  210.0 1.6 multiply_subtract_fusion
  211.6 11.1 %all_gather.14 = f32[192,1024]{1,0:T(8,128)S(1)} all-gather(f32[192,256]{1,0:T(8,128)S(1)} %get-tuple-element.2), channel_id=1, replica_groups=mesh['space'=4,'slot'=8] {'space'}, dimensions={1}, use_global_device_ids=true | all-gather | bytes 983040 | tf_op jit(solution)/shard_map/all_gather | solution.py:33
  223.4 1.1 bitcast_reduce_fusion
  224.6 1.0 copy_bitcast_fusion.2
  225.6 64.9 %all-gather.5.cloned.1.call-done = f32[1536,1024]{1,0:T(8,128)} async-done(((f32[192,1024]{1,0:T(8,128)}), f32[1536,1024]{1,0:T(8,128)}) %all-gather.5.cloned.1.call-update) | async-done | bytes 6291472 | tf_op jit(solution)/shard_map/all_gather | solution.py:48
  290.5 8.0 %convert_multiply_fusion.1 = f32[1536,1024]{1,0:T(8,128)} fusion(f32[1536,1024]{1,0:T(8,128)} %all-gather.5.cloned.1.call-done, bf16[1,1536,1024]{2,1,0:T(8,128)(2,1)} %param.11), kind=kLoop, calls=%fused_computation.3 | loop fusion | flops 3145728 | bytes 15728640 | tf_op jit(solution)/shard_map/mul | solution.py:49
  298.5 3.2 reduce_sum.63
  301.7 3.2 fusion.18
  304.9 4.2 %fusion = f32[48,1024]{1,0:T(8,128)S(1)} fusion(s32[2048]{0:T(1024)S(1)} %bitcast.116, f32[1,48,2048]{2,1,0:T(8,128)S(1)} %copy-done.7, f32[2048]{0:T(1024)S(1)} %bitcast.117), kind=kOutput, calls=%fused_computation.7 | convolution fusion | flops 1210155008 | bytes 606208 | tf_op jit(solution)/shard_map/dot_general | solution.py:44
  309.1 3.6 convert_multiply_fusion
  312.8 68.6 %reduce-scatter.9.cloned.1.call-done = f32[192,1024]{1,0:T(8,128)} async-done(((f32[1536,1024]{1,0:T(8,128)}), f32[192,1024]{1,0:T(8,128)}) %reduce-scatter.9.cloned.1.call-update) | async-done | bytes 786448 | tf_op jit(solution)/shard_map/reduce_scatter | solution.py:52
  381.3 1.3 copy.60
  383.4 1.5 fusion.14
  384.9 1.0 copy.76
  385.9 24.6 %reduce-scatter.11.cloned.1.call-done = f32[192,256]{1,0:T(8,128)} async-done(((f32[192,1024]{1,0:T(8,128)}), f32[192,256]{1,0:T(8,128)}) %reduce-scatter.11.cloned.1.call-update) | async-done | bytes 196624 | tf_op jit(solution)/shard_map/reduce_scatter | solution.py:69
  410.6 1.6 add.27
  (41 shorter events, 3.8 us)
Async XLA Ops:
  7.2 15.2 %copy-start = (bf16[8,2,128,128]{3,2,1,0:T(8,128)(2,1)S(1)}, bf16[8,2,128,128]{3,2,1,0:T(8,128)(2,1)}, u32[]{:S(2)}) copy-start(bf16[8,2,128,128]{3,2,1,0:T(8,128)(2,1)} %param.10) | copy-start | bytes 1572868
  7.2 82.6 %all-gather.3.cloned.1.call-start = ((), (), s32[]{:S(2)}) async-start(), calls=%async_computation.4 | async-start | bytes 7077888 | tf_op jit(solution)/shard_map/all_gather | solution.py:48
  22.4 2.2 copy-start.6
  24.6 156.2 %reduce-scatter.5.cloned.1.call-start = ((), (), s32[]{:S(2)}) async-start(), calls=%async_computation.5 | async-start | bytes 7077888 | tf_op jit(solution)/shard_map/reduce_scatter | solution.py:52
  97.8 3.3 copy-start.7
  101.0 3.2 copy-start.4
  101.0 3.2 copy-start.5
  101.1 7.5 %copy-start.1 = (bf16[1,1536,1024]{2,1,0:T(8,128)(2,1)S(1)}, bf16[1,1536,1024]{2,1,0:T(8,128)(2,1)}, u32[]{:S(2)}) copy-start(bf16[1,1536,1024]{2,1,0:T(8,128)(2,1)} %param.11) | copy-start | bytes 9437188
  112.1 97.9 %reduce-scatter.7.cloned.1.call-start = ((), (), s32[]{:S(2)}) async-start(), calls=%async_computation.6 | async-start | bytes 983040 | tf_op jit(solution)/shard_map/reduce_scatter | solution.py:69
  182.8 27.2 %copy-start.3 = (bf16[192,256]{1,0:T(8,128)(2,1)S(1)}, bf16[192,256]{1,0:T(8,128)(2,1)}, u32[]{:S(2)}) copy-start(bf16[192,256]{1,0:T(8,128)(2,1)} %param.8) | copy-start | bytes 294916
  185.4 105.1 %all-gather.5.cloned.1.call-start = ((), (), s32[]{:S(2)}) async-start(), calls=%async_computation.7 | async-start | bytes 7077888 | tf_op jit(solution)/shard_map/all_gather | solution.py:48
  225.6 155.7 %reduce-scatter.9.cloned.1.call-start = ((), (), s32[]{:S(2)}) async-start(), calls=%async_computation.8 | async-start | bytes 7077888 | tf_op jit(solution)/shard_map/reduce_scatter | solution.py:52
  301.7 7.4 %copy-start.2 = (bf16[1,1536,1024]{2,1,0:T(8,128)(2,1)S(1)}, bf16[1,1536,1024]{2,1,0:T(8,128)(2,1)}, u32[]{:S(2)}) copy-start(bf16[1,1536,1024]{2,1,0:T(8,128)(2,1)} %param.11) | copy-start | bytes 9437188
  312.7 97.9 %reduce-scatter.11.cloned.1.call-start = ((), (), s32[]{:S(2)}) async-start(), calls=%async_computation.9 | async-start | bytes 983040 | tf_op jit(solution)/shard_map/reduce_scatter | solution.py:69
Sparse Core Ops, SparseCore 0:
  24.7 65.0 all-gather.2
  112.2 68.4 reduce-scatter.4
  185.5 24.4 reduce-scatter.6
  225.7 64.7 all-gather.4
  312.8 68.4 reduce-scatter.8
  386.1 24.4 reduce-scatter.10
where the time goes:
time: 419 us
  waiting for transfers between devices  316 us (75%)
  other arithmetic  33.8 us (8%)
  blocking collectives  23.7 us (6%)
  matrix products  21.6 us (5%)
  between operations  14.4 us (3%)
  local copies, waits for them, and re-layouts  8.98 us (2%)
    reduce_scatter x2, waiting for transfers between devices, gradient(): lax.psum_scatter(own_slot.astype(jnp.float32) * jnp.tile(adjoint_obs, (me...  137 us
    all_gather x2, waiting for transfers between devices, gradient(): all_updates = lax.all_gather(updates, 'slot', axis=0, tiled=True)  130 us
    reduce_scatter x2, waiting for transfers between devices, gradient(): lax.psum_scatter(control_term.reshape(member_rows, block_total * BLOCK),...  49.2 us
    all_gather x2, blocking collectives, localize(): lax.all_gather(current.astype(jnp.float32), 'space', axis=1, tiled=True)  23.7 us
    mul x2, other arithmetic, gradient(): product_full = own_slot.astype(jnp.float32) * all_updates  16 us
    dot_general x2, matrix products, observe(): jnp.dot(weights * residual[None, :], pick_table.T, precision=lax.Precisio...  8.41 us
  transfers between devices with their start and end apart: 6, of which 6 were waited for; matrix products, arithmetic and copies ran while one was open for 0% of the time, Pallas kernels for 0%

commit v1 on v0

--- a/solution.py
+++ b/solution.py
@@ -30,7 +30,25 @@
     own_slot = ensemble[0]
 
     def localize(current):
-        gathered = lax.all_gather(current.astype(jnp.float32), "space", axis=1, tiled=True)
+        x = current.astype(jnp.float32)
+        devices, here, width = (lax.axis_size("space"), lax.axis_index("space"), x.shape[1])
+        right = [(i, (i + 1) % devices) for i in range(devices)]
+        left = [(i, (i - 1) % devices) for i in range(devices)]
+        out = jnp.zeros((*x.shape[:1], devices * width, *x.shape[1 + 1 :]), x.dtype)
+        out = lax.dynamic_update_slice_in_dim(out, x, here * width, axis=1)
+        from_left = from_right = x
+        middle = devices // 2
+        for step in range(1, middle + 1):
+            from_left = lax.ppermute(from_left, "space", right)
+            out = lax.dynamic_update_slice_in_dim(
+                out, from_left, (here - step) % devices * width, axis=1
+            )
+            if step < devices - middle:
+                from_right = lax.ppermute(from_right, "space", left)
+                out = lax.dynamic_update_slice_in_dim(
+                    out, from_right, (here + step) % devices * width, axis=1
+                )
+        gathered = out
         picked = gathered.reshape(member_rows, block_total, BLOCK)[:, ref_ids, :]
         products = jnp.einsum("crj,rij->cri", picked, tiles_flat, precision=lax.Precision.HIGHEST)
         return (

time: 419 us -> 428 us (1.021)
  blocking collectives: 23.7 us -> 0 us
  waiting for transfers between devices: 316 us -> 339 us
  starting transfers between devices: 0.43 us -> 9 us
    all_gather x2 -> x0, blocking collectives: 23.7 us -> none  [localize(): lax.all_gather(current.astype(jnp.float32), 'space', axis=1, tiled=True)]
    ppermute x0 -> x6, waiting for transfers between devices: none -> 22.6 us  [the longest x4 15.3 us: localize(): from_left = lax.ppermute(from_left, 'space', right)]
    ppermute x0 -> x6, starting transfers between devices: none -> 8.58 us  [the longest x4 6.07 us: localize(): from_left = lax.ppermute(from_left, 'space', right)]
  transfers between devices with their start and end apart: 6 -> 12, of which waited for: 6 -> 12; matrix products, arithmetic and copies ran while one was open for 0% -> 0% of each run, Pallas kernels for 0% -> 0%
where the time goes in v1:
time: 428 us
  waiting for transfers between devices  339 us (79%)
  other arithmetic  34.7 us (8%)
  matrix products  21.6 us (5%)
  between operations  14.5 us (3%)
  local copies, waits for them, and re-layouts  9.18 us (2%)
  starting transfers between devices  9 us (2%)
    reduce_scatter x2, waiting for transfers between devices, gradient(): lax.psum_scatter(own_slot.astype(jnp.float32) * jnp.tile(adjoint_obs, (me...  137 us
    all_gather x2, waiting for transfers between devices, gradient(): all_updates = lax.all_gather(updates, 'slot', axis=0, tiled=True)  130 us
    reduce_scatter x2, waiting for transfers between devices, gradient(): lax.psum_scatter(control_term.reshape(member_rows, block_total * BLOCK),...  49.2 us
    mul x2, other arithmetic, gradient(): product_full = own_slot.astype(jnp.float32) * all_updates  16 us
    ppermute x4, waiting for transfers between devices, localize(): from_left = lax.ppermute(from_left, 'space', right)  15.3 us
  transfers between devices with their start and end apart: 12, of which 12 were waited for; matrix products, arithmetic and copies ran while one was open for 0% of the time, Pallas kernels for 0%

profile of v1, /device:TPU:0, one launch (start us, length us, event | category | flops | bytes accessed | tf_op | source)
XLA Modules:
  0.0 428.0 jit_solution(12314878707856874715)
XLA Ops:
  8.2 3.0 collective-permute-start
  14.1 3.7 collective-permute-done
  19.0 3.7 collective-permute-done.1
  22.7 2.8 collective-permute-done.2
  26.2 1.1 bitcast_reduce_fusion.1
  28.4 65.4 %all-gather.3.cloned.1.call-done = f32[1536,1024]{1,0:T(8,128)} async-done(((f32[192,1024]{1,0:T(8,128)}), f32[1536,1024]{1,0:T(8,128)}) %all-gather.3.cloned.1.call-update) | async-done | bytes 6291472 | tf_op jit(solution)/shard_map/all_gather | solution.py:66
  93.8 8.0 %convert_multiply_fusion.3 = f32[1536,1024]{1,0:T(8,128)} fusion(f32[1536,1024]{1,0:T(8,128)} %all-gather.3.cloned.1.call-done, bf16[1,1536,1024]{2,1,0:T(8,128)(2,1)} %param.11), kind=kLoop, calls=%fused_computation.5 | loop fusion | flops 3145728 | bytes 15728640 | tf_op jit(solution)/shard_map/mul | solution.py:67
  101.8 3.2 reduce_sum.59
  105.1 3.2 fusion.19
  108.3 4.2 fusion.2
  112.6 3.5 convert_multiply_fusion.2
  116.4 68.3 %reduce-scatter.5.cloned.1.call-done = f32[192,1024]{1,0:T(8,128)} async-done(((f32[1536,1024]{1,0:T(8,128)}), f32[192,1024]{1,0:T(8,128)}) %reduce-scatter.5.cloned.1.call-update) | async-done | bytes 786448 | tf_op jit(solution)/shard_map/reduce_scatter | solution.py:70
  184.7 1.3 copy.58
  186.8 1.5 fusion.16
  189.4 24.5 %reduce-scatter.7.cloned.1.call-done = f32[192,256]{1,0:T(8,128)} async-done(((f32[192,1024]{1,0:T(8,128)}), f32[192,256]{1,0:T(8,128)}) %reduce-scatter.7.cloned.1.call-update) | async-done | bytes 196624 | tf_op jit(solution)/shard_map/reduce_scatter | solution.py:87
  214.1 1.7 constant_dynamic-update-slice_fusion.3
  215.7 1.4 collective-permute-start.3
  217.2 1.5 collective-permute-start.4
  218.7 5.8 %collective-permute-done.3 = f32[192,256]{1,0:T(8,128)S(1)} collective-permute-done((f32[192,256]{1,0:T(8,128)S(1)}, f32[192,256]{1,0:T(8,128)S(1)}, u32[]{:S(2)}, u32[]{:S(2)}) %collective-permute-start.3) | collective-permute-done | bytes 196640 | tf_op jit(solution)/shard_map/ppermute | solution.py:42
  225.0 3.6 collective-permute-done.4
  228.6 3.0 collective-permute-done.5
  234.6 64.8 %all-gather.5.cloned.1.call-done = f32[1536,1024]{1,0:T(8,128)} async-done(((f32[192,1024]{1,0:T(8,128)}), f32[1536,1024]{1,0:T(8,128)}) %all-gather.5.cloned.1.call-update) | async-done | bytes 6291472 | tf_op jit(solution)/shard_map/all_gather | solution.py:66
  299.4 8.0 %convert_multiply_fusion.1 = f32[1536,1024]{1,0:T(8,128)} fusion(f32[1536,1024]{1,0:T(8,128)} %all-gather.5.cloned.1.call-done, bf16[1,1536,1024]{2,1,0:T(8,128)(2,1)} %param.11), kind=kLoop, calls=%fused_computation.3 | loop fusion | flops 3145728 | bytes 15728640 | tf_op jit(solution)/shard_map/mul | solution.py:67
  307.4 3.2 reduce_sum.63
  310.6 3.2 fusion.18
  313.8 4.2 fusion
  318.1 3.5 convert_multiply_fusion
  321.7 68.6 %reduce-scatter.9.cloned.1.call-done = f32[192,1024]{1,0:T(8,128)} async-done(((f32[1536,1024]{1,0:T(8,128)}), f32[192,1024]{1,0:T(8,128)}) %reduce-scatter.9.cloned.1.call-update) | async-done | bytes 786448 | tf_op jit(solution)/shard_map/reduce_scatter | solution.py:70
  390.2 1.3 copy.60
  392.3 1.5 fusion.14
  394.9 24.6 %reduce-scatter.11.cloned.1.call-done = f32[192,256]{1,0:T(8,128)} async-done(((f32[192,1024]{1,0:T(8,128)}), f32[192,256]{1,0:T(8,128)}) %reduce-scatter.11.cloned.1.call-update) | async-done | bytes 196624 | tf_op jit(solution)/shard_map/reduce_scatter | solution.py:87
  419.5 1.6 add.70
  (60 shorter events, 14.4 us)
Async XLA Ops:
  7.2 19.0 %copy-start = (bf16[8,2,128,128]{3,2,1,0:T(8,128)(2,1)S(1)}, bf16[8,2,128,128]{3,2,1,0:T(8,128)(2,1)}, u32[]{:S(2)}) copy-start(bf16[8,2,128,128]{3,2,1,0:T(8,128)(2,1)} %param.10) | copy-start | bytes 1572868
  7.2 86.6 %all-gather.3.cloned.1.call-start = ((), (), s32[]{:S(2)}) async-start(), calls=%async_computation.4 | async-start | bytes 7077888 | tf_op jit(solution)/shard_map/all_gather | solution.py:66
  8.2 9.7 %collective-permute-start = (f32[192,256]{1,0:T(8,128)S(1)}, f32[192,256]{1,0:T(8,128)S(1)}, u32[]{:S(2)}, u32[]{:S(2)}) collective-permute-start(f32[192,256]{1,0:T(8,128)S(1)} %convert_element_type.7), channel_id=1, source_target_pairs={{0,8},{8,16},{16,24},{24,0},{1,9},{9,17},{17,25},{25,1},{2,10},{10... | collective-permute-start | bytes 589832 | tf_op jit(solution)/shard_map/ppermute | solution.py:42
  11.2 11.5 %collective-permute-start.1 = (f32[192,256]{1,0:T(8,128)S(1)}, f32[192,256]{1,0:T(8,128)S(1)}, u32[]{:S(2)}, u32[]{:S(2)}) collective-permute-start(f32[192,256]{1,0:T(8,128)S(1)} %convert_element_type.7), channel_id=1, source_target_pairs={{0,24},{8,0},{16,8},{24,16},{1,25},{9,1},{17,9},{25,17},{2,26},{10... | collective-permute-start | bytes 589832 | tf_op jit(solution)/shard_map/ppermute | solution.py:47
  17.9 7.6 %collective-permute-start.2 = (f32[192,256]{1,0:T(8,128)S(1)}, f32[192,256]{1,0:T(8,128)S(1)}, u32[]{:S(2)}, u32[]{:S(2)}) collective-permute-start(f32[192,256]{1,0:T(8,128)S(1)} %collective-permute-done), channel_id=1, source_target_pairs={{0,8},{8,16},{16,24},{24,0},{1,9},{9,17},{17,25},{25,1},{2,10},{10... | collective-permute-start | bytes 589832 | tf_op jit(solution)/shard_map/ppermute | solution.py:42
  26.2 2.2 copy-start.6
  28.3 156.4 %reduce-scatter.5.cloned.1.call-start = ((), (), s32[]{:S(2)}) async-start(), calls=%async_computation.5 | async-start | bytes 7077888 | tf_op jit(solution)/shard_map/reduce_scatter | solution.py:70
  101.8 3.3 copy-start.7
  105.0 3.3 copy-start.4
  105.1 3.2 copy-start.5
  105.1 7.5 %copy-start.1 = (bf16[1,1536,1024]{2,1,0:T(8,128)(2,1)S(1)}, bf16[1,1536,1024]{2,1,0:T(8,128)(2,1)}, u32[]{:S(2)}) copy-start(bf16[1,1536,1024]{2,1,0:T(8,128)(2,1)} %param.11) | copy-start | bytes 9437188
  116.1 97.9 %reduce-scatter.7.cloned.1.call-start = ((), (), s32[]{:S(2)}) async-start(), calls=%async_computation.6 | async-start | bytes 983040 | tf_op jit(solution)/shard_map/reduce_scatter | solution.py:87
  188.3 25.8 %copy-start.3 = (bf16[192,256]{1,0:T(8,128)(2,1)S(1)}, bf16[192,256]{1,0:T(8,128)(2,1)}, u32[]{:S(2)}) copy-start(bf16[192,256]{1,0:T(8,128)(2,1)} %param.8) | copy-start | bytes 294916
  189.4 110.0 %all-gather.5.cloned.1.call-start = ((), (), s32[]{:S(2)}) async-start(), calls=%async_computation.7 | async-start | bytes 7077888 | tf_op jit(solution)/shard_map/all_gather | solution.py:66
  215.7 8.7 %collective-permute-start.3 = (f32[192,256]{1,0:T(8,128)S(1)}, f32[192,256]{1,0:T(8,128)S(1)}, u32[]{:S(2)}, u32[]{:S(2)}) collective-permute-start(f32[192,256]{1,0:T(8,128)S(1)} %get-tuple-element.3), channel_id=1, source_target_pairs={{0,8},{8,16},{16,24},{24,0},{1,9},{9,17},{17,25},{25,1},{2,10},{10... | collective-permute-start | bytes 589832 | tf_op jit(solution)/shard_map/ppermute | solution.py:42
  217.2 11.4 %collective-permute-start.4 = (f32[192,256]{1,0:T(8,128)S(1)}, f32[192,256]{1,0:T(8,128)S(1)}, u32[]{:S(2)}, u32[]{:S(2)}) collective-permute-start(f32[192,256]{1,0:T(8,128)S(1)} %get-tuple-element.3), channel_id=1, source_target_pairs={{0,24},{8,0},{16,8},{24,16},{1,25},{9,1},{17,9},{25,17},{2,26},{10... | collective-permute-start | bytes 589832 | tf_op jit(solution)/shard_map/ppermute | solution.py:47
  224.4 7.3 %collective-permute-start.5 = (f32[192,256]{1,0:T(8,128)S(1)}, f32[192,256]{1,0:T(8,128)S(1)}, u32[]{:S(2)}, u32[]{:S(2)}) collective-permute-start(f32[192,256]{1,0:T(8,128)S(1)} %collective-permute-done.3), channel_id=1, source_target_pairs={{0,8},{8,16},{16,24},{24,0},{1,9},{9,17},{17,25},{25,1},{2,10},{10... | collective-permute-start | bytes 589832 | tf_op jit(solution)/shard_map/ppermute | solution.py:42
  234.5 155.7 %reduce-scatter.9.cloned.1.call-start = ((), (), s32[]{:S(2)}) async-start(), calls=%async_computation.8 | async-start | bytes 7077888 | tf_op jit(solution)/shard_map/reduce_scatter | solution.py:70
  310.6 7.4 %copy-start.2 = (bf16[1,1536,1024]{2,1,0:T(8,128)(2,1)S(1)}, bf16[1,1536,1024]{2,1,0:T(8,128)(2,1)}, u32[]{:S(2)}) copy-start(bf16[1,1536,1024]{2,1,0:T(8,128)(2,1)} %param.11) | copy-start | bytes 9437188
  321.6 97.9 %reduce-scatter.11.cloned.1.call-start = ((), (), s32[]{:S(2)}) async-start(), calls=%async_computation.9 | async-start | bytes 983040 | tf_op jit(solution)/shard_map/reduce_scatter | solution.py:87
Sparse Core Ops, SparseCore 0:
  28.5 65.2 all-gather.2
  116.2 68.4 reduce-scatter.4
  189.5 24.4 reduce-scatter.6
  234.7 64.7 all-gather.4
  321.7 68.4 reduce-scatter.8
  395.0 24.4 reduce-scatter.10
